TPU v7x, 32 devices: a whole 2x2x4 slice. The times are simulated.
32 devices in a mesh: blk: 8 (over z, y), smp: 4 (over x, core).
Axes of the slice: x: 2, y: 2, z: 4, core: 2. Of those that a mesh axis runs over, the one named last changes fastest.
Arguments:
- forward_samples: bfloat16 [256, 65536], P('smp', 'blk'), may hold values from -0.375 to 0.375
- adjoint_samples: bfloat16 [256, 16384], P('smp', 'blk'), may hold values from -0.125 to 0.125
- probe_values: bfloat16 [16384, 192], P('blk'), may hold values from -6 to 6
- owners: int32 [16384, 1], P('blk'), may hold values from 0 to 7; in each aligned block of 2048 rows (0 to 2047, 2048 to 4095, ...) at most 512 rows name the same one
- block_ranks: int32 [8], P('blk'), may hold values from 64 to 256
- twiddle: float32 [2, 65536], P(None, 'blk'), may hold values from -1.2 to 1.2
Outputs:
- applied: bfloat16 [192, 65536], P('smp', 'blk')
Inputs may be any that keep to these rules, and one draw needn't show every extreme that they name: `owners`: in the rows of one block index no owner block is named more than 512 times.
All inputs are finite; a program needn't handle non-finite values.
Results may differ from a plain program's by a relative error of at most 0.005.
Values may be sent and summed in bfloat16 or wider, within the bound.
A program may use at most 64 MiB of HBM per device.

v0:
```python
import functools

import jax
import jax.numpy as jnp
from jax import lax
from jax.experimental import pallas as pl
from jax.experimental.pallas import tpu as pltpu
from jax.sharding import PartitionSpec as P

CHUNKS = 2
STAGES = (2, 3, 4)


def kernel(
    blocks, smp, fwd, adj_in, probe_in, tw_in, owners_in, ranks, out,
    adj, probe, owners, part, part_in, piece, piece_in, across, across_in, gathered, left, limits,
    xbuf, twbuf, obuf,
    load_sem, part_send, part_recv, piece_send, piece_recv,
    col_send, col_recv, limit_send, limit_recv, x_send, x_recv, x_own,
    tw_send, tw_recv, tw_own, o_send, o_recv, o_own,
):
    levels = tw_in.shape[0]
    group = 2 ** levels
    low_count = blocks // group
    samples = fwd.shape[0]
    vectors = probe_in.shape[0]
    vlocal = vectors // smp
    span = fwd.shape[1] // (group * smp)
    chunks, width = xbuf.shape[0], xbuf.shape[2]
    depth = group * samples
    blk, j = lax.axis_index("blk"), lax.axis_index("smp")
    h, low = blk // low_count, blk % low_count
    rank = h * smp + j
    odd = h % 2
    pair = h + 1 - 2 * odd

    def up_h(d):
        return (h + d) % group

    def up_j(d):
        return (j + d) % smp

    def dev(hh, ll, jj):
        return {"blk": hh * low_count + ll, "smp": jj}

    def remote(src, dst, send, recv, where):
        return pltpu.make_async_remote_copy(
            src_ref=src, dst_ref=dst, send_sem=send, recv_sem=recv,
            device_id=where, device_id_type=pl.DeviceIdType.MESH,
        )

    shifts = [(dh, dj) for dh in range(group) for dj in range(smp)]
    far = [s for s in shifts if s != (0, 0)]
    far.sort(key=lambda s: (-min(s[0], group - s[0]), s[0], s[1]))

    loads = [
        pltpu.make_async_copy(src, dst, load_sem.at[i])
        for i, (src, dst) in enumerate(((owners_in, owners), (adj_in, adj), (probe_in, probe)))
    ]
    for c in loads:
        c.start()

    barrier = pltpu.get_barrier_semaphore()
    for dh, dj in far:
        pl.semaphore_signal(
            barrier, inc=1, device_id=dev(up_h(dh), low, up_j(dj)),
            device_id_type=pl.DeviceIdType.MESH,
        )
    for d in range(1, low_count):
        pl.semaphore_signal(
            barrier, inc=1, device_id=dev(h, (low + d) % low_count, j),
            device_id_type=pl.DeviceIdType.MESH,
        )
    def aligned(start, size):
        return pl.ds(pl.multiple_of(start, size), size)

    for c in loads:
        c.wait()

    def partial_sums(lo):
        stacked = jnp.concatenate(
            [
                adj[...] * (owners[...] == hh * low_count + lo).astype(jnp.bfloat16)
                for hh in range(group)
            ],
            axis=0,
        )
        part[lo] = lax.dot_general(
            probe[...], stacked, (((1,), (1,)), ((), ())), preferred_element_type=jnp.float32
        )

    if low_count > 2:
        lax.fori_loop(0, low_count, lambda lo, c: (partial_sums(lo), c)[1], 0)
    else:
        for lo in range(low_count):
            partial_sums(lo)
    limits[h] = jnp.full(limits.shape[1:], ranks[0].astype(jnp.float32))

    pl.semaphore_wait(barrier, len(far) + low_count - 1)

    def part_copy(d):
        lo = (low + d) % low_count
        return remote(
            part.at[lo], part_in.at[d], part_send.at[d], part_recv.at[d], dev(h, lo, j)
        )

    def send_part(d, carry):
        part_copy(d).start()
        return carry

    if low_count > 1:
        lax.fori_loop(1, low_count, send_part, 0)

    def x_copy(k, dh, dj):
        to = up_h(dh) * smp + up_j(dj)
        src = fwd.at[:, aligned(to * span + k * width, width)]
        dst = xbuf.at[k, aligned(j * depth + h * samples, samples), :]
        if (dh, dj) == (0, 0):
            return pltpu.make_async_copy(src, dst, x_own.at[k])
        index = dh * smp + dj
        return remote(
            src, dst, x_send.at[k, index], x_recv.at[k, index], dev(up_h(dh), low, up_j(dj))
        )

    turns = sorted(range(group), key=lambda d: (d == 0, abs(2 * d - group)))
    x_units = [(k, dh) for k in range(chunks) for dh in turns]
    x_copies = {k: [] for k in range(chunks)}

    def send_x(first, last):
        for k, dh in x_units[first:last]:
            for dj in range(smp):
                c = x_copy(k, dh, dj)
                c.start()
                x_copies[k].append(c)

    send_x(0, STAGES[0])
    tw_copies = []
    for dh in range(group):
        src = tw_in.at[:, aligned((up_h(dh) * smp + j) * span, span)]
        dst = twbuf.at[h]
        if dh == 0:
            tw_copies.append(pltpu.make_async_copy(src, dst, tw_own))
        else:
            tw_copies.append(
                remote(src, dst, tw_send.at[dh], tw_recv.at[dh], dev(up_h(dh), low, j))
            )
            tw_copies.append(
                remote(
                    limits.at[h], limits.at[h], limit_send.at[dh], limit_recv.at[dh],
                    dev(up_h(dh), low, j),
                )
            )
    for c in tw_copies:
        c.start()

    total = part.at[low]

    def add_part(d, carry):
        part_copy(d).wait()
        total[...] += part_in[d]
        return carry

    if low_count > 1:
        lax.fori_loop(1, low_count, add_part, 0)

    half = vectors // 2
    mine, theirs = aligned(odd * half, half), aligned((1 - odd) * half, half)
    piece[...] = total[theirs, :].astype(jnp.bfloat16)
    pair_copy = remote(
        piece, piece_in, piece_send.at[0], piece_recv.at[0], dev(pair, low, j)
    )
    pair_copy.start()
    send_x(STAGES[0], STAGES[1])
    pair_copy.wait()
    coeffs = total[mine, :] + piece_in[...].astype(jnp.float32)
    across[...] = coeffs.astype(jnp.bfloat16)
    across_copy = remote(
        across, across_in, piece_send.at[1], piece_recv.at[1], dev(up_h(group // 2), low, j)
    )
    across_copy.start()
    send_x(STAGES[1], STAGES[2])
    across_copy.wait()
    coeffs += across_in[...].astype(jnp.float32)
    gathered[j, mine, :] = coeffs.astype(jnp.bfloat16)
    own = gathered.at[j, mine, :]
    col_copies = {
        (dp, dj): remote(
            own, own, col_send.at[dp, dj], col_recv.at[dp, dj],
            dev((h, pair)[dp], low, up_j(dj)),
        )
        for dj in range(smp) for dp in range(2) if (dp, dj) != (0, 0)
    }
    for c in col_copies.values():
        c.start()
    send_x(STAGES[2], len(x_units))
    for c in tw_copies:
        c.wait()
    lane = lax.broadcasted_iota(jnp.int32, (1, depth), 1)

    def spread(jj):
        number = (jj * samples + lane % samples).astype(jnp.float32)
        for hh in range(group):
            keep = (lane // samples == hh) & (number < limits[hh, 0:1, 0:1])
            left[hh * vectors : (hh + 1) * vectors, aligned(jj * depth, depth)] = (
                gathered[jj] * keep.astype(jnp.bfloat16)
            )

    for dj in range(smp):
        for dp in range(2):
            if (dp, dj) in col_copies:
                col_copies[dp, dj].wait()
        spread((j + smp - dj) % smp)

    o_copies = []
    for k in range(chunks):
        for c in x_copies[k]:
            c.wait()
        product = jnp.dot(left[...], xbuf[k], preferred_element_type=jnp.float32)
        field = [product[hh * vectors : (hh + 1) * vectors] for hh in range(group)]
        for level in range(levels):
            distance = group >> (level + 1)
            field = [
                field[hh]
                + twbuf[hh, level : level + 1, k * width : (k + 1) * width]
                * field[hh ^ distance]
                for hh in range(group)
            ]
        for hh in range(group):
            obuf[k, hh] = field[hh].astype(jnp.bfloat16)
        cols = aligned(rank * span + k * width, width)
        for dh, dj in far + [(0, 0)]:
            src = obuf.at[k, up_h(dh), aligned(up_j(dj) * vlocal, vlocal), :]
            dst = out.at[:, cols]
            if (dh, dj) == (0, 0):
                c = pltpu.make_async_copy(src, dst, o_own.at[k])
            else:
                index = dh * smp + dj
                c = remote(
                    src, dst, o_send.at[k, index], o_recv.at[k, index],
                    dev(up_h(dh), low, up_j(dj)),
                )
            c.start()
            o_copies.append(c)
    for c in o_copies:
        c.wait()


def body(blocks, smp, fwd, adj, probe, owners, ranks, twiddle):
    samples, box = fwd.shape
    rows, vectors = probe.shape
    levels = twiddle.shape[0]
    group = 2 ** levels
    low_count = blocks // group
    peers = group * smp
    span = box // peers
    chunks = CHUNKS
    width = span // chunks
    depth = group * samples
    dma = pltpu.SemaphoreType.DMA
    hbm = pl.BlockSpec(memory_space=pltpu.HBM)
    return pl.pallas_call(
        functools.partial(kernel, blocks, smp),
        out_shape=jax.ShapeDtypeStruct((vectors // smp, box), jnp.bfloat16),
        in_specs=[
            hbm, hbm, hbm, hbm, hbm,
            pl.BlockSpec(memory_space=pltpu.SMEM),
        ],
        out_specs=hbm,
        scratch_shapes=[
            pltpu.VMEM(adj.shape, jnp.bfloat16),
            pltpu.VMEM((vectors, rows), jnp.bfloat16),
            pltpu.VMEM((1, rows), jnp.int32),
            pltpu.VMEM((low_count, vectors, depth), jnp.float32),
            pltpu.VMEM((low_count, vectors, depth), jnp.float32),
            pltpu.VMEM((vectors // 2, depth), jnp.bfloat16),
            pltpu.VMEM((vectors // 2, depth), jnp.bfloat16),
            pltpu.VMEM((vectors // 2, depth), jnp.bfloat16),
            pltpu.VMEM((vectors // 2, depth), jnp.bfloat16),
            pltpu.VMEM((smp, vectors, depth), jnp.bfloat16),
            pltpu.VMEM((group * vectors, smp * depth), jnp.bfloat16),
            pltpu.VMEM((group, 8, 128), jnp.float32),
            pltpu.VMEM((chunks, smp * depth, width), jnp.bfloat16),
            pltpu.VMEM((group, levels, span), jnp.float32),
            pltpu.VMEM((chunks, group, vectors, width), jnp.bfloat16),
            dma((3,)),
            dma((low_count,)), dma((low_count,)),
            dma((2,)), dma((2,)),
            dma((2, smp)), dma((2, smp)),
            dma((group,)), dma((group,)),
            dma((chunks, peers)), dma((chunks, peers)), dma((chunks,)),
            dma((group,)), dma((group,)), dma,
            dma((chunks, peers)), dma((chunks, peers)), dma((chunks,)),
        ],
        compiler_params=pltpu.CompilerParams(
            collective_id=0, has_side_effects=True, vmem_limit_bytes=67_000_000
        ),
        name="butterfly",
    )(fwd, adj, probe.T, twiddle, owners.reshape(1, rows), ranks)


def solution(mesh):
    in_specs = (
        P("smp", "blk"),
        P("smp", "blk"),
        P("blk", None),
        P("blk", None),
        P("blk"),
        P(None, "blk"),
    )
    return jax.shard_map(
        functools.partial(body, mesh.shape["blk"], mesh.shape["smp"]),
        mesh=mesh, in_specs=in_specs, out_specs=P("smp", "blk"), check_vma=False,
    )
```

profile of v0, /device:TPU:0, one launch (start us, length us, event | category | flops | bytes accessed | tf_op | source)
XLA Modules:
  0.0 53.8 jit_solution(14586183087818816667)
XLA Ops:
  0.7 51.1 %butterfly.1 = bf16[48,8192]{1,0:T(8,128)(2,1)} custom-call(bf16[64,8192]{1,0:T(8,128)(2,1)} %fwd.1, bf16[64,2048]{1,0:T(8,128)(2,1)} %adj_in.1, bf16[192,2048]{1,0:T(8,128)(2,1)} %bitcast.2, f32[2,8192]{1,0:T(2,128)} %tw_in.1, s32[1,2048]{1,0:T(1,128)} %bitcast.3, s32[1]{0:T(128)S(6)} %copy.8.ranks), custom_call_target="tpu_custom_call" | custom-call | tf_op jit(solution)/shard_map/butterfly/pallas_call | solution.py:261
  51.7 2.1 %copy.9 = bf16[48,8192]{1,0:T(8,128)(2,1)} copy(bf16[48,8192]{1,0:T(8,128)(2,1)} %butterfly.1) | data formatting | bytes 1572864
where the time goes:
time: 54 us; the launch traced here: 53.8 us
  Pallas kernels  51.1 us (95%)
  local copies, waits for them, and re-layouts  2.06 us (4%)
  between operations  0.66 us (1%)
    pallas_call x1, Pallas kernels, body(): pl.pallas_call(functools.partial(kernel, blocks, smp), out_shape=jax.Shap...  51.1 us
    unnamed x1, local copies, waits for them, and re-layouts  2.06 us

commit v1 on v0

v1 whole, which is shorter than its diff:
```python
import functools

import jax
import jax.numpy as jnp
from jax import lax
from jax.experimental import pallas as pl
from jax.experimental.pallas import tpu as pltpu
from jax.sharding import PartitionSpec as P

DIRECT = 256
WIDTH = 128
EARLY = 2
MESH = pl.DeviceIdType.MESH


def kernel(
    blocks, smp, fwd, adj_in, probe_in, tw_in, owners_in, ranks, out,
    adj, probe, owners, mine, psend, precv, acr, acr_in, gath, left, limits,
    xa, fb, fs, fr, tw, oa, ob,
    load_sem, chain, p_send, p_recv, c_send, c_recv, g_send, g_recv, t_send, t_recv,
    xa_send, xa_recv, fb_send, fb_recv, f_send, f_recv, oa_send, oa_recv, ob_send, ob_recv,
    own_sem,
):
    levels = tw_in.shape[0]
    group = 2 ** levels
    low_count = blocks // group
    samples = fwd.shape[0]
    vectors = probe_in.shape[0]
    vlocal = vectors // smp
    wa = xa.shape[2]
    chunks, wc = fr.shape[0], fr.shape[3]
    wb = chunks * wc
    half = 2 * samples
    blk, j = lax.axis_index("blk"), lax.axis_index("smp")
    h, low = blk // low_count, blk % low_count
    q = h % 2
    inner = ((h + 1) // 2) % 2
    near, opp, diag = h + 1 - 2 * q, (h + 2) % group, group - 1 - h
    block_at = (h, near, opp, diag)
    rank = h * smp + j
    base = group * smp * wa

    def up(d):
        return (j + d) % smp

    def dev(hh, ll, jj):
        return {"blk": hh * low_count + ll, "smp": jj}

    def aligned(start, size):
        return pl.ds(pl.multiple_of(start, size), size)

    def remote(src, dst, send, recv, where):
        return pltpu.make_async_remote_copy(
            src_ref=src, dst_ref=dst, send_sem=send, recv_sem=recv,
            device_id=where, device_id_type=MESH,
        )

    def each(first, last, step):
        if last - first > 2:
            lax.fori_loop(first, last, lambda d, c: (step(d), c)[1], 0)
        else:
            for d in range(first, last):
                step(d)

    loads = [
        pltpu.make_async_copy(src, dst, load_sem.at[i])
        for i, (src, dst) in enumerate(((owners_in, owners), (adj_in, adj), (probe_in, probe)))
    ]
    for c in loads:
        c.start()

    barrier = pltpu.get_barrier_semaphore()

    def signal(sem, where):
        pl.semaphore_signal(sem, inc=1, device_id=where, device_id_type=MESH)

    def greet(hh):
        for dj in range(smp):
            signal(barrier, dev(hh, low, up(dj)))

    below, above = h > 0, h < group - 1
    sides = jnp.where(below, 1, 0) + jnp.where(above, 1, 0)
    pl.when(above)(lambda: greet(h + 1))
    pl.when(below)(lambda: greet(h - 1))
    for dj in range(1, smp):
        signal(barrier, dev(h, low, up(dj)))

    def greet_low(d):
        lo = (low + d) % low_count
        signal(barrier, dev(h, lo, j))
        signal(barrier, dev(near, lo, j))

    each(1, low_count, greet_low)

    def pass_on(sem):
        pl.when(above)(lambda: signal(sem, dev(h + 1, low, j)))
        pl.when(below)(lambda: signal(sem, dev(h - 1, low, j)))

    def fa_copy(x, hh, dj):
        to = hh * smp + up(dj)
        slot = x * smp + dj
        return remote(
            fwd.at[:, aligned(to * wa, wa)], xa.at[h, aligned(j * samples, samples), :],
            xa_send.at[slot], xa_recv.at[slot], dev(hh, low, up(dj)),
        )

    first_x, second_x = 1 + 2 * inner, 3 - 2 * inner
    first_h = inner * diag + (1 - inner) * near
    second_h = inner * near + (1 - inner) * diag
    fa = {
        "first": [fa_copy(first_x, first_h, dj) for dj in range(smp)],
        "opp": [fa_copy(2, opp, dj) for dj in range(smp)],
        "second": [fa_copy(second_x, second_h, dj) for dj in range(smp)],
        "own": [fa_copy(0, h, dj) for dj in range(1, smp)],
    }

    def fb_copy(d):
        return remote(
            fwd.at[:, aligned(base + up(d) * group * wb, group * wb)],
            fb.at[aligned(j * samples, samples), :],
            fb_send.at[d], fb_recv.at[d], dev(h, low, up(d)),
        )

    fb_copies = [fb_copy(d) for d in range(1, smp)]
    owned = [
        pltpu.make_async_copy(
            fwd.at[:, aligned(rank * wa, wa)], xa.at[h, aligned(j * samples, samples), :],
            own_sem.at[0],
        ),
        pltpu.make_async_copy(
            fwd.at[:, aligned(base + j * group * wb, group * wb)],
            fb.at[aligned(j * samples, samples), :], own_sem.at[1],
        ),
    ]

    pl.semaphore_wait(barrier, smp * sides + smp - 1 + 2 * (low_count - 1))
    pass_on(chain.at[0])

    def begin(copies):
        for c in copies:
            c.start()

    pl.when(inner == 1)(lambda: begin(fa["first"]))
    for c in loads:
        c.wait()

    def partial_sums(lo):
        stacked = jnp.concatenate(
            [
                adj[...] * (owners[...] == hh * low_count + lo).astype(jnp.bfloat16)
                for side in range(2)
                for hh in range(side, group, 2)
            ],
            axis=0,
        )
        return lax.dot_general(
            probe[...], stacked, (((1,), (1,)), ((), ())), preferred_element_type=jnp.float32
        )

    def part_copy(d, side):
        where = dev((h, near)[side], (low + d) % low_count, j)
        mark = q if side == 0 else 1 - q
        return remote(
            psend.at[d, mark], precv.at[d, side], p_send.at[d, side], p_recv.at[d, side], where
        )

    def send_parts(d):
        total = partial_sums((low + d) % low_count)
        for side in range(2):
            psend[d, side] = total[:, side * half : (side + 1) * half].astype(jnp.bfloat16)
        part_copy(d, 0).start()
        part_copy(d, 1).start()

    each(1, low_count, send_parts)
    total = partial_sums(low)
    for side in range(2):
        piece = total[:, side * half : (side + 1) * half]
        mine[side] = piece
        psend[0, side] = piece.astype(jnp.bfloat16)
    part_copy(0, 1).start()
    limits[0] = jnp.full(limits.shape[1:], ranks[0].astype(jnp.float32))

    pl.semaphore_wait(chain.at[0], sides)
    pass_on(chain.at[1])
    limit_copy = remote(
        limits.at[0], limits.at[1], t_send.at[0, 0], t_recv.at[0, 0], dev(opp, low, j)
    )
    limit_copy.start()

    @pl.when(inner == 1)
    def _():
        begin(fa["opp"][:EARLY])
        begin(fa["second"])

    pl.when(inner == 0)(lambda: begin(fa["first"]))
    begin(owned)
    begin(fb_copies)

    small = []
    for x in range(group):
        hh = block_at[x]
        for i, (start, size, at) in enumerate((
            ((hh * smp + j) * wa, wa, 0), (base + (j * group + hh) * wb, wb, wa),
        )):
            src, dst = tw_in.at[:, aligned(start, size)], tw.at[h, :, at : at + size]
            if x == 0:
                small.append(pltpu.make_async_copy(src, dst, own_sem.at[2 + i]))
            else:
                small.append(
                    remote(src, dst, t_send.at[x, i], t_recv.at[x, i], dev(hh, low, j))
                )
    part_copy(0, 1).wait()
    mine[q] += precv[0, 1].astype(jnp.float32)

    def add_parts(d):
        for side in range(2):
            part_copy(d, side).wait()
        mine[q] += precv[d, 0].astype(jnp.float32) + precv[d, 1].astype(jnp.float32)

    each(1, low_count, add_parts)
    acr[...] = mine[q].astype(jnp.bfloat16)
    acr_copy = remote(acr, acr_in, c_send, c_recv, dev(opp, low, j))
    acr_copy.start()
    pl.when(inner == 1)(lambda: begin(fa["opp"][EARLY:]))
    pl.semaphore_wait(chain.at[1], sides)
    limit_copy.wait()

    lane = lax.broadcasted_iota(jnp.int32, (1, half), 1)
    number = (j * samples + lane % samples).astype(jnp.float32)
    limit = jnp.where(
        lane // samples == h // 2, limits[0, 0:1, 0:1], limits[1, 0:1, 0:1]
    )
    keep = (number < limit).astype(jnp.float32)
    acr_copy.wait()
    gath[q, j] = ((mine[q] + acr_in[...].astype(jnp.float32)) * keep).astype(jnp.bfloat16)

    def gath_copy(x, dj):
        return remote(
            gath.at[q, j], gath.at[q, j], g_send.at[x, dj], g_recv.at[x, dj],
            dev(block_at[x], low, up(dj)),
        )

    same = [gath_copy(0, dj) for dj in range(1, smp)]
    cross = [gath_copy(1, dj) for dj in range(smp)]
    begin(same)

    @pl.when(inner == 0)
    def _():
        begin(fa["opp"])
        begin(fa["second"])

    begin(cross)
    begin(fa["own"])
    begin(small)

    def build(side):
        front = lane < samples
        for jj in range(0, smp, 2):
            a = gath[side, jj].astype(jnp.float32)
            b = gath[side, jj + 1].astype(jnp.float32)
            cols = slice(jj * samples, (jj + 2) * samples)
            left[side, :, cols] = jnp.where(front, a, pltpu.roll(b, samples, 1)).astype(
                jnp.bfloat16
            )
            left[side + 2, :, cols] = jnp.where(front, pltpu.roll(a, samples, 1), b).astype(
                jnp.bfloat16
            )

    for c in owned + fb_copies + same:
        c.wait()
    build(q)

    f_copies = {}
    for k in range(chunks):
        for x in (2, 3, 1, 0):
            hh = block_at[x]
            product = jnp.dot(
                left[h], fb[:, aligned(hh * wb + k * wc, wc)], preferred_element_type=jnp.float32
            ).astype(jnp.bfloat16)
            if x == 0:
                fr[k, h] = product
                continue
            fs[k, x] = product
            f_copies[k, x] = remote(
                fs.at[k, x], fr.at[k, h], f_send.at[k, x], f_recv.at[k, x], dev(hh, low, j)
            )
            f_copies[k, x].start()

    def butterfly(field, at):
        for level in range(levels):
            distance = group >> (level + 1)
            field = [
                field[hh] + tw[hh, level : level + 1, at : at + wc] * field[hh ^ distance]
                for hh in range(group)
            ]
        return field

    sent = []

    def send_out(src, cols, send, recv, spare):
        for x in (2, 3, 1, 0):
            for dj in range(smp):
                piece = src.at[block_at[x], aligned(up(dj) * vlocal, vlocal), :]
                dst = out.at[:, cols]
                if (x, dj) == (0, 0):
                    c = pltpu.make_async_copy(piece, dst, spare)
                else:
                    slot = x * smp + dj
                    c = remote(
                        piece, dst, send.at[slot], recv.at[slot], dev(block_at[x], low, up(dj))
                    )
                c.start()
                sent.append(c)

    for c in cross:
        c.wait()
    build(1 - q)
    for name in fa:
        for c in fa[name]:
            c.wait()
    for c in small:
        c.wait()
    for at in range(0, wa, wc):
        field = [
            jnp.dot(left[hh], xa[hh, :, at : at + wc], preferred_element_type=jnp.float32)
            for hh in range(group)
        ]
        field = butterfly(field, at)
        for hh in range(group):
            oa[hh, :, at : at + wc] = field[hh].astype(jnp.bfloat16)
    send_out(oa, aligned(rank * wa, wa), oa_send, oa_recv, own_sem.at[4])
    for k in range(chunks):
        for x in (1, 2, 3):
            f_copies[k, x].wait()
        field = butterfly([fr[k, hh].astype(jnp.float32) for hh in range(group)], wa + k * wc)
        for hh in range(group):
            ob[k, hh] = field[hh].astype(jnp.bfloat16)
        cols = aligned(base + (j * group + h) * wb + k * wc, wc)
        send_out(ob.at[k], cols, ob_send.at[k], ob_recv.at[k], own_sem.at[5 + k])
    for c in sent:
        c.wait()


def body(blocks, smp, fwd, adj, probe, owners, ranks, twiddle):
    samples, box = fwd.shape
    rows, vectors = probe.shape
    levels = twiddle.shape[0]
    group = 2 ** levels
    low_count = blocks // group
    peers = group * smp
    span = box // peers
    wa, wc = DIRECT, WIDTH
    wb = span - wa
    chunks = wb // wc
    half = 2 * samples
    bf16, f32 = jnp.bfloat16, jnp.float32
    dma = pltpu.SemaphoreType.DMA
    hbm = pl.BlockSpec(memory_space=pltpu.HBM)
    result = 2 * (vectors // smp) * box
    return pl.pallas_call(
        functools.partial(kernel, blocks, smp),
        out_shape=pltpu.VMEM((vectors // smp, box), bf16),
        in_specs=[
            hbm, hbm, hbm, hbm, hbm,
            pl.BlockSpec(memory_space=pltpu.SMEM),
        ],
        out_specs=pl.BlockSpec(memory_space=pltpu.VMEM),
        scratch_shapes=[
            pltpu.VMEM(adj.shape, bf16),
            pltpu.VMEM((vectors, rows), bf16),
            pltpu.VMEM((1, rows), jnp.int32),
            pltpu.VMEM((2, vectors, half), f32),
            pltpu.VMEM((low_count, 2, vectors, half), bf16),
            pltpu.VMEM((low_count, 2, vectors, half), bf16),
            pltpu.VMEM((vectors, half), bf16),
            pltpu.VMEM((vectors, half), bf16),
            pltpu.VMEM((2, smp, vectors, half), bf16),
            pltpu.VMEM((group, vectors, smp * samples), bf16),
            pltpu.VMEM((2, 8, 128), f32),
            pltpu.VMEM((group, smp * samples, wa), bf16),
            pltpu.VMEM((smp * samples, group * wb), bf16),
            pltpu.VMEM((chunks, group, vectors, wc), bf16),
            pltpu.VMEM((chunks, group, vectors, wc), bf16),
            pltpu.VMEM((group, levels, span), f32),
            pltpu.VMEM((group, vectors, wa), bf16),
            pltpu.VMEM((chunks, group, vectors, wc), bf16),
            dma((3,)), pltpu.SemaphoreType.REGULAR((2,)),
            dma((low_count, 2)), dma((low_count, 2)),
            dma, dma,
            dma((2, smp)), dma((2, smp)),
            dma((group, 2)), dma((group, 2)),
            dma((peers,)), dma((peers,)),
            dma((smp,)), dma((smp,)),
            dma((chunks, group)), dma((chunks, group)),
            dma((peers,)), dma((peers,)),
            dma((chunks, peers)), dma((chunks, peers)),
            dma((5 + chunks,)),
        ],
        compiler_params=pltpu.CompilerParams(
            collective_id=0, has_side_effects=True, vmem_limit_bytes=67_030_000 - result
        ),
        name="butterfly",
    )(fwd, adj, probe.T, twiddle, owners.reshape(1, rows), ranks)


def solution(mesh):
    in_specs = (
        P("smp", "blk"),
        P("smp", "blk"),
        P("blk", None),
        P("blk", None),
        P("blk"),
        P(None, "blk"),
    )
    return jax.shard_map(
        functools.partial(body, mesh.shape["blk"], mesh.shape["smp"]),
        mesh=mesh, in_specs=in_specs, out_specs=P("smp", "blk"), check_vma=False,
    )
```

time: 54 us -> 51.9 us (0.961)
  local copies, waits for them, and re-layouts: 2.06 us -> 0.88 us
  Pallas kernels: 51.1 us -> 50.2 us
    unnamed x1, local copies, waits for them, and re-layouts: 2.06 us -> 0.88 us
    pallas_call x1, Pallas kernels: 51.1 us -> 50.2 us  [body(): pl.pallas_call(functools.partial(kernel, blocks, smp), out_shape=pltpu.VM...]
where the time goes in v1:
time: 51.9 us; the launch traced here: 51.7 us
  Pallas kernels  50.2 us (97%)
  local copies, waits for them, and re-layouts  0.88 us (2%)
  between operations  0.66 us (1%)
    pallas_call x1, Pallas kernels, body(): pl.pallas_call(functools.partial(kernel, blocks, smp), out_shape=pltpu.VM...  50.2 us

profile of v1, /device:TPU:0, one launch (start us, length us, event | category | flops | bytes accessed | tf_op | source)
XLA Modules:
  0.0 51.7 jit_solution(10747568615143866637)
XLA Ops:
  0.7 50.2 %butterfly.1 = bf16[48,8192]{1,0:T(8,128)(2,1)S(1)} custom-call(bf16[64,8192]{1,0:T(8,128)(2,1)} %fwd.1, bf16[64,2048]{1,0:T(8,128)(2,1)} %adj_in.1, bf16[192,2048]{1,0:T(8,128)(2,1)} %bitcast.2, f32[2,8192]{1,0:T(2,128)} %tw_in.1, s32[1,2048]{1,0:T(1,128)} %bitcast.3, s32[1]{0:T(128)S(6)} %copy.9.ranks), custom_call_target="tpu_custom_call" | custom-call | tf_op jit(solution)/shard_map/butterfly/pallas_call | solution.py:360
  50.9 0.9 %copy.8 = bf16[48,8192]{1,0:T(8,128)(2,1)} copy(bf16[48,8192]{1,0:T(8,128)(2,1)S(1)} %butterfly.1) | data formatting | bytes 1572864
